TPU v7x, 32 devices: a whole 2x2x4 slice. The times are simulated.
32 devices in a mesh: dp: 8 (over z, x), tensor: 4 (over y, core).
Axes of the slice: x: 2, y: 2, z: 4, core: 2. Of those that a mesh axis runs over, the one named last changes fastest.
Arguments:
- inputs: bfloat16 [16, 1024, 1024], P('dp'), may hold values from -6 to 6
- segment_ids: int32 [16, 1024], P('dp'), may hold values from 0 to 7, never falling along the last dimension, each value on 1 to 512 neighbouring positions
- doc_offsets: int32 [16, 8], P('dp'), may hold values from 0 to 3071
- time_index: int32 [16], P('dp'), may hold values from 0 to 999
- w_qkv: bfloat16 [3, 1024, 1024], P(None, 'dp', 'tensor'), may hold values from -0.1875 to 0.1875
- w_out: bfloat16 [1024, 1024], P('tensor', 'dp'), may hold values from -0.75 to 0.75
- w_up: bfloat16 [1024, 4096], P('dp', 'tensor'), may hold values from -0.1875 to 0.1875
- w_down: bfloat16 [4096, 1024], P('tensor', 'dp'), may hold values from -0.09375 to 0.09375
- w_time: bfloat16 [256, 1024], P(None, 'dp'), may hold values from -0.375 to 0.375
- gain_attn: bfloat16 [1024], P('dp'), may hold values from 0.5 to 1.5
- gain_mlp: bfloat16 [1024], P('dp'), may hold values from 0.5 to 1.5
- cotangent: bfloat16 [16, 1024, 1024], P('dp'), may hold values from -6 to 6
Outputs:
- block_out: bfloat16 [16, 1024, 1024], P('dp', None, 'tensor')
- input_grad: float32 [16, 1024, 1024], P('dp', None, 'tensor')
- grad_qkv: float32 [3, 1024, 1024], P(None, 'dp', 'tensor')
- grad_out: float32 [1024, 1024], P('tensor', 'dp')
- grad_up: float32 [1024, 4096], P('dp', 'tensor')
- grad_down: float32 [4096, 1024], P('tensor', 'dp')
- grad_time: float32 [256, 1024], P(None, 'dp')
- grad_gain_attn: float32 [1024], P('dp')
- grad_gain_mlp: float32 [1024], P('dp')
Inputs may be any that keep to these rules, and one draw needn't show every extreme that they name: `segment_ids`: in each sequence the ids never fall, every id of 0 to 7 occurs, each document has 1 to 512 tokens and one has exactly 512.
All inputs are finite; a program needn't handle non-finite values.
Results may differ from a plain program's by a relative error of at most 0.022.
Values may be sent and summed in bfloat16 or wider, within the bound.
No kernel may reach another device: no remote copies, remote signals or barrier semaphores. Data moves between devices by JAX's collectives and lax.ppermute only.
A program may use at most 192 MiB of HBM per device.

v0:
```python
import math
import jax
import jax.numpy as jnp
from jax import lax
from jax.sharding import PartitionSpec as P

HEADS = 16
TEMB = 256
eps = 1e-05
masked = -1000000000.0
f32 = jnp.float32
bf16 = jnp.bfloat16


def sinusoid(values, width):
    half = width // 2
    freqs = jnp.exp(-math.log(10000.0) * jnp.arange(half, dtype=f32) / half)
    angles = values[..., None] * freqs
    return jnp.concatenate([jnp.sin(angles), jnp.cos(angles)], axis=-1)


def norm_parts(hidden):
    centre = jnp.mean(hidden, axis=-1, keepdims=True)
    centred = hidden - centre
    spread = jnp.mean(centred * centred, axis=-1, keepdims=True)
    inv = lax.rsqrt(spread + eps)
    return (centred * inv, inv)


def norm_back(unit, inv, gain, grad):
    scaled = grad * gain
    first = jnp.mean(scaled, axis=-1, keepdims=True)
    second = jnp.mean(scaled * unit, axis=-1, keepdims=True)
    return inv * (scaled - first - unit * second)


def positions(segs, offsets):
    seq_len = segs.shape[0]
    index = jnp.arange(seq_len, dtype=jnp.int32)
    member = segs[:, None] == jnp.arange(offsets.shape[0], dtype=jnp.int32)[None, :]
    starts = jnp.min(jnp.where(member, index[:, None], seq_len), axis=0)
    start_tok = jnp.sum(jnp.where(member, starts[None, :], 0), axis=1)
    offset_tok = jnp.sum(jnp.where(member, offsets[None, :], 0), axis=1)
    return offset_tok + index - start_tok


def attend(query, key, value, same, scale):
    scores = jnp.einsum("qhe,khe->hqk", query, key, preferred_element_type=f32) * scale
    scores = jnp.where(same[None], scores, masked)
    top = jnp.max(scores, axis=-1, keepdims=True)
    expo = jnp.exp(scores - top)
    denom = jnp.sum(expo, axis=-1, keepdims=True)
    probs = (expo / denom).astype(bf16)
    out = jnp.einsum("hqk,khe->qhe", probs, value, preferred_element_type=f32)
    return (out, top + jnp.log(denom))


def attend_back(query, key, value, same, scale, lse, d_mixed):
    scores = jnp.einsum("qhe,khe->hqk", query, key, preferred_element_type=f32) * scale
    scores = jnp.where(same[None], scores, masked)
    probs = jnp.exp(scores - lse)
    d_probs = jnp.einsum("qhe,khe->hqk", d_mixed, value, preferred_element_type=f32)
    d_value = jnp.einsum("hqk,qhe->khe", probs.astype(bf16), d_mixed, preferred_element_type=f32)
    delta = jnp.sum(probs * d_probs, axis=-1, keepdims=True)
    d_scores = (probs * (d_probs - delta)).astype(bf16)
    d_query = jnp.einsum("hqk,khe->qhe", d_scores, key, preferred_element_type=f32) * scale
    d_key = jnp.einsum("hqk,qhe->khe", d_scores, query, preferred_element_type=f32) * scale
    return (d_query, d_key, d_value)


def mm(left, right):
    return jnp.dot(left, right, preferred_element_type=f32)


def mm_rt(left, right):
    return jnp.einsum("ik,jk->ij", left, right, preferred_element_type=f32)


def mm_lt(left, right):
    return jnp.einsum("ki,kj->ij", left, right, preferred_element_type=f32)


class Ring:

    def __init__(self, n):
        self.n = n
        self.order = list(range(0, n, 2)) + list(range(n - 1, 0, -2))
        inverse = [self.order.index(i) for i in range(n)]
        self.me = lax.axis_index("dp")
        self.spot = jnp.array(inverse, jnp.int32)[self.me]
        self.table = jnp.array(self.order, jnp.int32)
        self.right = [(self.order[p], self.order[(p + 1) % n]) for p in range(n)]
        self.left = [(b, a) for a, b in self.right]

    def at(self, offset):
        return self.table[(self.spot + offset) % self.n]

    def gather(self, block):
        rows = block.shape[0]
        full = jnp.zeros((self.n * rows,) + block.shape[1:], block.dtype)
        full = lax.dynamic_update_slice_in_dim(full, block, self.me * rows, 0)
        from_left = from_right = block
        for hop in range(1, self.n // 2 + 1):
            from_left = lax.ppermute(from_left, "dp", self.right)
            if hop <= self.n - 1 - self.n // 2:
                from_right = lax.ppermute(from_right, "dp", self.left)
                full = lax.dynamic_update_slice_in_dim(full, from_right, self.at(hop) * rows, 0)
            full = lax.dynamic_update_slice_in_dim(full, from_left, self.at(-hop) * rows, 0)
        return full

    def scatter(self, full):
        rows = full.shape[0] // self.n

        def part(offset):
            return lax.dynamic_slice_in_dim(full, self.at(offset) * rows, rows, 0).astype(f32)

        total = part(0)
        for hops, way, sign in (
            (self.n // 2, self.right, 1),
            (self.n - 1 - self.n // 2, self.left, -1),
        ):
            run = part(sign * hops)
            for hop in range(1, hops + 1):
                run = lax.ppermute(run.astype(bf16), "dp", way).astype(f32)
                if hop < hops:
                    run = run + part(sign * (hops - hop))
            if hops:
                total = total + run
        return total


def swap(value, bit, n):
    return lax.ppermute(value, "tensor", [(i, i ^ bit) for i in range(n)])


def to_features(value, n):
    me = lax.axis_index("tensor")
    tokens, width = value.shape
    value = value.reshape(tokens, n, width // n)
    bit = 1
    while bit < n:
        value = value.reshape(tokens, -1, 2, width // n)
        mine = me // bit % 2
        keep = lax.dynamic_index_in_dim(value, mine, 2, keepdims=False)
        send = lax.dynamic_index_in_dim(value, 1 - mine, 2, keepdims=False)
        got = swap(send.astype(bf16), bit, n).astype(f32)
        if bit == 1:
            got = jnp.concatenate([got[tokens // 2 :], got[: tokens // 2]], axis=0)
        value = keep.astype(f32) + got
        bit *= 2
    return value.reshape(tokens, width // n)


def shards(
    inputs,
    segment_ids,
    doc_offsets,
    time_index,
    w_qkv,
    w_out,
    w_up,
    w_down,
    w_time,
    gain_attn,
    gain_mlp,
    cotangent,
):
    n_dp = lax.axis_size("dp")
    n_tensor = lax.axis_size("tensor")
    me_dp = lax.axis_index("dp")
    core = lax.axis_index("tensor") % 2
    chips = n_tensor // 2
    seqs_dev, seq_len, width = inputs.shape
    half = seq_len // 2
    shard = width // n_tensor
    head_size = width // HEADS
    heads_dev = shard // head_size
    scale = head_size ** (-0.5)
    hidden_dev = w_up.shape[1]
    ring = Ring(n_dp)
    w1_part = jnp.concatenate([w_qkv[0], w_qkv[1], w_qkv[2], w_out.T], axis=1)
    w1 = ring.gather(w1_part)
    w2_part = jnp.concatenate([w_up, w_down.T], axis=1)
    w2 = lax.all_gather(w2_part, "dp", axis=0, tiled=True)
    times = lax.all_gather(time_index, "dp", axis=0, tiled=True)
    temb = sinusoid(times.astype(f32), TEMB)
    cond_part = jnp.dot(temb, w_time.astype(f32), precision=lax.Precision.HIGHEST)
    small = jnp.concatenate(
        [cond_part, gain_attn.astype(f32)[None], gain_mlp.astype(f32)[None]], axis=0
    )
    small = lax.all_gather(small, "dp", axis=1, tiled=True)
    n_seqs = n_dp * seqs_dev
    cond = lax.dynamic_slice_in_dim(small, me_dp * seqs_dev, seqs_dev, 0)
    attn_g, mlp_g = (small[n_seqs], small[n_seqs + 1])

    def own_first(value):
        return jnp.roll(value, -core * half, axis=0)

    def exchange_core(value):
        return swap(value, 1, n_tensor)

    def sum_chips(value):
        bit = 2
        value = value.astype(f32)
        while bit < n_tensor:
            low = value.astype(bf16)
            value = low.astype(f32) + swap(low, bit, n_tensor).astype(f32)
            bit *= 2
        return value

    seqs = range(seqs_dev)
    cot = [own_first(cotangent[i]) for i in seqs]
    segs = [own_first(segment_ids[i]) for i in seqs]
    same = [s[:, None] == s[None, :] for s in segs]
    h0, unit0, inv0, n1 = ([], [], [], [])
    for i in seqs:
        place = own_first(positions(segment_ids[i], doc_offsets[i]))
        h = own_first(inputs[i]).astype(f32) + sinusoid(place.astype(f32), width) + cond[i][None]
        unit, inv = norm_parts(h)
        h0.append(h)
        unit0.append(unit)
        inv0.append(inv)
        n1.append((unit * attn_g).astype(bf16))
    query, key, value, mixed, lse = ([], [], [], [], [])
    h1, unit1, inv1, n2 = ([], [], [], [])
    for i in seqs:
        qkv = mm(n1[i], w1[:, : 3 * shard]).astype(bf16)
        heads = [
            qkv[:, c * shard : (c + 1) * shard].reshape(seq_len, heads_dev, head_size)
            for c in range(3)
        ]
        out, total = attend(*heads, same[i], scale)
        out = out.reshape(seq_len, shard).astype(bf16)
        send = mm_rt(out[half:], w1[:, 3 * shard :]).astype(bf16)
        keep = mm_rt(out[:half], w1[:, 3 * shard :]).astype(bf16)
        attn = sum_chips(keep.astype(f32) + exchange_core(send).astype(f32))
        h = h0[i][:half] + attn
        unit, inv = norm_parts(h)
        own = (unit * mlp_g).astype(bf16)
        query.append(heads[0])
        key.append(heads[1])
        value.append(heads[2])
        mixed.append(out)
        lse.append(total)
        h1.append(h)
        unit1.append(unit)
        inv1.append(inv)
        n2.append(jnp.concatenate([own, exchange_core(own)], axis=0))
    w_up_full, w_down_t = (w2[:, :hidden_dev], w2[:, hidden_dev:])
    active, d_hidden, d_h1, d_h1_low, block_out = ([], [], [], [], [])
    gain_mlp_sum = jnp.zeros((width,), f32)
    for i in seqs:
        hidden = mm(n2[i], w_up_full)
        d_active = mm(cot[i], w_down_t)
        erf = lax.erf(hidden * 0.5**0.5)
        cdf = 0.5 + 0.5 * erf
        active.append((hidden * cdf).astype(bf16))
        slope = cdf + hidden * jnp.exp(-0.5 * hidden * hidden) * (0.5 / math.pi) ** 0.5
        d_hidden.append((d_active * slope).astype(bf16))
        d_n2_send = mm_rt(d_hidden[i][half:], w_up_full).astype(bf16)
        d_n2_keep = mm_rt(d_hidden[i][:half], w_up_full).astype(bf16)
        d_n2 = sum_chips(d_n2_keep.astype(f32) + exchange_core(d_n2_send).astype(f32))
        gain_mlp_sum = gain_mlp_sum + jnp.sum(d_n2 * unit1[i], axis=0)
        d_h1.append(cot[i][:half].astype(f32) + norm_back(unit1[i], inv1[i], mlp_g, d_n2))
        low = d_h1[i].astype(bf16)
        d_h1_low.append(jnp.concatenate([low, exchange_core(low)], axis=0))
        term = mm_rt(active[i], w_down_t)
        term = jnp.concatenate([term[:half] + h1[i] * (1.0 / chips), term[half:]], axis=0)
        block_out.append(to_features(term.astype(bf16), n_tensor).astype(bf16))
    cot_all = jnp.concatenate(cot, axis=0)
    grad2 = jnp.concatenate(
        [
            mm_lt(jnp.concatenate(n2, axis=0), jnp.concatenate(d_hidden, axis=0)).astype(bf16),
            mm_lt(cot_all, jnp.concatenate(active, axis=0)).astype(bf16),
        ],
        axis=1,
    )
    share2 = lax.psum_scatter(grad2, "dp", scatter_dimension=0, tiled=True).astype(f32)
    d_qkv, input_grad, seq_sums = ([], [], [])
    gain_attn_sum = jnp.zeros((width,), f32)
    for i in seqs:
        d_mixed = mm(d_h1_low[i], w1[:, 3 * shard :]).astype(bf16)
        parts = attend_back(
            query[i],
            key[i],
            value[i],
            same[i],
            scale,
            lse[i],
            d_mixed.reshape(seq_len, heads_dev, head_size),
        )
        d_qkv.append(
            jnp.concatenate([p.reshape(seq_len, shard).astype(bf16) for p in parts], axis=1)
        )
        d_n1 = mm_rt(d_qkv[i], w1[:, : 3 * shard])
        gain_attn_sum = gain_attn_sum + jnp.sum(d_n1 * unit0[i], axis=0)
        term = norm_back(unit0[i], inv0[i], attn_g, d_n1)
        term = jnp.concatenate([term[:half] + d_h1[i] * (1.0 / chips), term[half:]], axis=0)
        seq_sums.append(jnp.sum(term, axis=0))
        input_grad.append(to_features(term.astype(bf16), n_tensor))
    grad1 = jnp.concatenate(
        [
            mm_lt(jnp.concatenate(n1, axis=0), jnp.concatenate(d_qkv, axis=0)).astype(bf16),
            mm_lt(jnp.concatenate(d_h1_low, axis=0), jnp.concatenate(mixed, axis=0)).astype(bf16),
        ],
        axis=1,
    )
    share1 = ring.scatter(grad1)
    sums = jnp.zeros((n_seqs, width), f32)
    sums = lax.dynamic_update_slice_in_dim(sums, jnp.stack(seq_sums), me_dp * seqs_dev, 0)
    sums = jnp.concatenate([sums, gain_attn_sum[None], gain_mlp_sum[None] * (1.0 / chips)], axis=0)
    sums = lax.psum(sums, ("dp", "tensor"))
    rows = width // n_dp
    sums = lax.dynamic_slice_in_dim(sums, me_dp * rows, rows, 1)
    factor = float(n_seqs * seq_len) ** (-0.5)
    grad_time = (
        jnp.einsum("st,sd->td", temb, sums[:n_seqs], precision=lax.Precision.HIGHEST) * factor
    )

    def natural(value):
        return jnp.roll(value, core * half, axis=0)

    share1, share2 = (share1 * factor, share2 * factor)
    return (
        jnp.stack([natural(b) for b in block_out]),
        jnp.stack([natural(g) for g in input_grad]),
        jnp.stack([share1[:, c * shard : (c + 1) * shard] for c in range(3)]),
        share1[:, 3 * shard :].T,
        share2[:, :hidden_dev],
        share2[:, hidden_dev:].T,
        grad_time,
        sums[n_seqs] * factor,
        sums[n_seqs + 1] * factor,
    )


def solution(mesh):
    in_specs = (
        P("dp", None, None),
        P("dp", None),
        P("dp", None),
        P("dp"),
        P(None, "dp", "tensor"),
        P("tensor", "dp"),
        P("dp", "tensor"),
        P("tensor", "dp"),
        P(None, "dp"),
        P("dp"),
        P("dp"),
        P("dp", None, None),
    )
    out_specs = (
        P("dp", None, "tensor"),
        P("dp", None, "tensor"),
        P(None, "dp", "tensor"),
        P("tensor", "dp"),
        P("dp", "tensor"),
        P("tensor", "dp"),
        P(None, "dp"),
        P("dp"),
        P("dp"),
    )
    return jax.shard_map(shards, mesh=mesh, in_specs=in_specs, out_specs=out_specs, check_vma=False)
```

profile of v0, /device:TPU:0, one launch (start us, length us, event | category | flops | bytes accessed | tf_op | source)
XLA Modules:
  0.0 683.9 jit_solution(16655282718602888327)
XLA Ops:
  14.9 12.1 %all-reduce = s32[16]{0:T(128)S(1)} all-reduce(s32[16]{0:T(128)S(1)} %dynamic-update-slice), channel_id=1, replica_groups=mesh['dp'=8,'tensor'=4] {'dp'}, use_global_device_ids=true, to_apply=%add | all-reduce | flops 16 | bytes 128
  28.4 31.2 %all_gather.10 = f32[18,1024]{1,0:T(8,128)S(1)} all-gather(f32[18,128]{1,0:T(8,128)S(1)} %pad_maximum_fusion.10), channel_id=1, replica_groups=mesh['dp'=8,'tensor'=4] {'dp'}, dimensions={1}, use_global_device_ids=true | all-gather | bytes 82944 | tf_op jit(solution)/shard_map/all_gather | solution.py:191
  64.4 16.2 %multiply_sine_fusion.1 = (f32[1024,512]{1,0:T(8,128)S(1)}, f32[1024,512]{1,0:T(8,128)S(1)}, f32[1024,512]{1,0:T(8,128)}, f32[1024,512]{1,0:T(8,128)}) fusion(f32[512]{0:T(512)S(1)} %multiply_exponential_fusion, f32[1024]{0:T(1024)S(1)} %get-tuple-element.168, f32[1024]{0:T(1024)S(1)} %get-tuple-element.166), kind=kLoop, calls=%fused_computation.119 | loop fusion | flops 1048576 | bytes 8398848 | tf_op jit(solution)/shard_map/sin | solution.py:19
  118.0 7.5 %fusion.238 = (f32[4,1024]{1,0:T(4,128)S(1)}, f32[4,1024,1024]{1,2,0:T(8,128)}) fusion(bf16[1024,4,64]{0,2,1:T(8,128)(2,1)S(1)} %bitcast.178, bf16[1024,4,64]{0,2,1:T(8,128)(2,1)S(1)} %bitcast.176, pred[1024,1024]{0,1:T(8,128)(4,1)S(1)} %broadcast_compare_fusion.1), kind=kOutput, calls=%fused_computation.439 | convolution fusion | flops 549449728 | bytes 18890752 | tf_op jit(solution)/shard_map/qhe,khe->hqk/dot_general | solution.py:48
  125.5 8.0 %fusion = f32[4,1024]{1,0:T(4,128)S(1)} fusion(f32[4,1024,1024]{1,2,0:T(8,128)} %get-tuple-element.152, f32[4,1024]{1,0:T(4,128)S(1)} %get-tuple-element.151), kind=kLoop, calls=%fused_computation.12 | loop fusion | flops 8384512 | bytes 16809984 | tf_op jit(solution)/shard_map/reduce_sum | solution.py:52
  133.5 7.6 %fusion.144 = bf16[4,64,1024]{2,1,0:T(8,128)(2,1)S(1)} fusion(bf16[1024,4,64]{0,2,1:T(8,128)(2,1)S(1)} %bitcast.188, f32[4,1024,1024]{1,2,0:T(8,128)} %get-tuple-element.152, f32[4,1024]{1,0:T(4,128)S(1)} %fusion, f32[4,1024]{1,0:T(4,128)S(1)} %get-tuple-element.151), kind=kOutput, calls=%fused_computation.250 | convolution fusion | flops 549715968 | bytes 17858560 | tf_op jit(solution)/shard_map/hqk,khe->qhe/dot_general | solution.py:54
  146.3 23.7 %collective-permute-done.8 = bf16[512,1024]{1,0:T(8,128)(2,1)S(1)} collective-permute-done((bf16[512,1024]{1,0:T(8,128)(2,1)S(1)}, bf16[512,1024]{1,0:T(8,128)(2,1)S(1)}, u32[]{:S(2)}, u32[]{:S(2)}) %collective-permute-start.8) | collective-permute-done | bytes 1048608 | tf_op jit(solution)/shard_map/ppermute | solution.py:133
  206.0 12.1 %collective-permute-done.18 = bf16[512,1024]{1,0:T(8,128)(2,1)} collective-permute-done((bf16[512,1024]{1,0:T(8,128)(2,1)S(1)}, bf16[512,1024]{1,0:T(8,128)(2,1)}, u32[]{:S(2)}, u32[]{:S(2)}) %collective-permute-start.18) | collective-permute-done | bytes 1048608 | tf_op jit(solution)/shard_map/ppermute | solution.py:133
  229.7 9.4 %fusion.124 = bf16[4,64,1024]{2,1,0:T(8,128)(2,1)} fusion(bf16[1024,4,64]{0,2,1:T(8,128)(2,1)S(1)} %bitcast.182, f32[4,1024,1024]{1,2,0:T(8,128)} %get-tuple-element.152, f32[4,1024]{1,0:T(4,128)S(1)} %log_add_fusion.1), kind=kOutput, calls=%fused_computation.240 | convolution fusion | flops 545521664 | bytes 17842176 | tf_op jit(solution)/shard_map/hqk,qhe->khe/dot_general | solution.py:63
  239.1 7.6 %multiply_reduce_fusion.1 = (f32[4,1024]{1,0:T(4,128)S(1)}, f32[4,1024,1024]{1,2,0:T(8,128)}) fusion(f32[4,1024,1024]{1,2,0:T(8,128)S(1)} %bitcast.171, f32[4,1024]{1,0:T(4,128)S(1)} %log_add_fusion.1, bf16[1024,4,64]{0,2,1:T(8,128)(2,1)S(1)} %bitcast.183, bf16[1024,4,64]{0,2,1:T(8,128)(2,1)S(1)} %bitcast.189), kind=kOutput, calls=%fused_computation.4 | convolution fusion | flops 549449728 | bytes 34635776 | tf_op jit(solution)/shard_map/qhe,khe->hqk/dot_general | solution.py:62
  246.7 8.3 %multiply_convert_fusion.1 = bf16[4,1024,1024]{1,2,0:T(8,128)(2,1)S(1)} fusion(f32[4,1024,1024]{1,2,0:T(8,128)} %get-tuple-element.156, f32[4,1024,1024]{1,2,0:T(8,128)S(1)} %bitcast.171, f32[4,1024]{1,0:T(4,128)S(1)} %get-tuple-element.155, f32[4,1024]{1,0:T(4,128)S(1)} %log_add_fusion.1), kind=kLoop, calls=%fused_computation.3 | loop fusion | flops 16777216 | bytes 41975808 | tf_op jit(solution)/shard_map/convert_element_type | solution.py:65
  270.1 7.5 %fusion.239 = (f32[4,1024]{1,0:T(4,128)S(1)}, f32[4,1024,1024]{1,2,0:T(8,128)}) fusion(bf16[1024,4,64]{0,2,1:T(8,128)(2,1)S(1)} %bitcast.174, bf16[1024,4,64]{0,2,1:T(8,128)(2,1)S(1)} %bitcast.172, pred[1024,1024]{0,1:T(8,128)(4,1)S(1)} %broadcast_compare_fusion), kind=kOutput, calls=%fused_computation.440 | convolution fusion | flops 549449728 | bytes 18890752 | tf_op jit(solution)/shard_map/qhe,khe->hqk/dot_general | solution.py:48
  277.5 8.0 %fusion.1 = f32[4,1024]{1,0:T(4,128)S(1)} fusion(f32[4,1024,1024]{1,2,0:T(8,128)} %get-tuple-element.159, f32[4,1024]{1,0:T(4,128)S(1)} %get-tuple-element.158), kind=kLoop, calls=%fused_computation.13 | loop fusion | flops 8384512 | bytes 16809984 | tf_op jit(solution)/shard_map/reduce_sum | solution.py:52
  285.6 7.7 %fusion.143 = bf16[4,64,1024]{2,1,0:T(8,128)(2,1)S(1)} fusion(bf16[1024,4,64]{0,2,1:T(8,128)(2,1)S(1)} %bitcast.186, f32[4,1024,1024]{1,2,0:T(8,128)} %get-tuple-element.159, f32[4,1024]{1,0:T(4,128)S(1)} %fusion.1, f32[4,1024]{1,0:T(4,128)S(1)} %get-tuple-element.158), kind=kOutput, calls=%fused_computation.249 | convolution fusion | flops 549715968 | bytes 17858560 | tf_op jit(solution)/shard_map/hqk,khe->qhe/dot_general | solution.py:54
  298.5 23.7 %collective-permute-done.13 = bf16[512,1024]{1,0:T(8,128)(2,1)S(1)} collective-permute-done((bf16[512,1024]{1,0:T(8,128)(2,1)S(1)}, bf16[512,1024]{1,0:T(8,128)(2,1)S(1)}, u32[]{:S(2)}, u32[]{:S(2)}) %collective-permute-start.13) | collective-permute-done | bytes 1048608 | tf_op jit(solution)/shard_map/ppermute | solution.py:133
  380.8 9.4 %fusion.89 = bf16[1024,1024]{0,1:T(8,128)(2,1)} fusion(bf16[1024,1024]{1,0:T(8,128)(2,1)} %get-tuple-element.160, bf16[1024,1024]{1,0:T(8,128)(2,1)} %copy-done.109, bf16[1024,1024]{1,0:T(8,128)(2,1)} %fusion.67, bf16[1024,1024]{1,0:T(8,128)(2,1)} %fusion.68), kind=kOutput, calls=%fused_computation.203 | convolution fusion | flops 4312793088 | bytes 10485760 | tf_op jit(solution)/shard_map/ki,kj->ij/dot_general | solution.py:80
  403.2 9.2 %fusion.94 = bf16[1024,1024]{0,1:T(8,128)(2,1)} fusion(bf16[1024,1024]{1,0:T(8,128)(2,1)} %copy-done.108, bf16[1024,1024]{1,0:T(8,128)(2,1)} %copy-done.107, bf16[512,1024]{1,0:T(8,128)(2,1)} %collective-permute-done.14, bf16[512,1024]{1,0:T(8,128)(2,1)} %multiply_convert_fusion.6, bf16[512,1024]{1,0:T(8,128)(2,1)} %collective-permute-done.9, ...), kind=kOutput, calls=%fused_computation.204 | convolution fusion | flops 4321181696 | bytes 10485760 | tf_op jit(solution)/shard_map/ki,kj->ij/dot_general | solution.py:80
  419.0 10.5 %multiply_reduce_fusion = (f32[4,1024]{1,0:T(4,128)S(1)}, f32[4,1024,1024]{1,2,0:T(8,128)}) fusion(f32[4,1024,1024]{1,2,0:T(8,128)S(1)} %bitcast.169, f32[4,1024]{1,0:T(4,128)S(1)} %log_add_fusion, bf16[1024,4,64]{0,2,1:T(8,128)(2,1)} %bitcast.185, bf16[1024,4,64]{0,2,1:T(8,128)(2,1)} %bitcast.187), kind=kOutput, calls=%fused_computation.1 | convolution fusion | flops 549449728 | bytes 34635776 | tf_op jit(solution)/shard_map/qhe,khe->hqk/dot_general | solution.py:62
  429.6 8.0 %multiply_convert_fusion = bf16[4,1024,1024]{1,2,0:T(8,128)(2,1)S(1)} fusion(f32[4,1024,1024]{1,2,0:T(8,128)} %get-tuple-element.163, f32[4,1024,1024]{1,2,0:T(8,128)S(1)} %bitcast.169, f32[4,1024]{1,0:T(4,128)S(1)} %get-tuple-element.162, f32[4,1024]{1,0:T(4,128)S(1)} %log_add_fusion), kind=kLoop, calls=%fused_computation | loop fusion | flops 16777216 | bytes 41975808 | tf_op jit(solution)/shard_map/convert_element_type | solution.py:65
  483.2 7.7 %collective-permute-done.21 = bf16[1024,1,256]{2,0,1:T(8,128)(2,1)} collective-permute-done((bf16[1024,1,256]{2,0,1:T(8,128)(2,1)}, bf16[1024,1,256]{2,0,1:T(8,128)(2,1)}, u32[]{:S(2)}, u32[]{:S(2)}) %collective-permute-start.21) | collective-permute-done | bytes 524320 | tf_op jit(solution)/shard_map/ppermute | solution.py:133
  520.4 49.7 %all-reduce.3.cloned.1.call-done = f32[18,1024]{1,0:T(8,128)} async-done(((f32[18,1024]{1,0:T(8,128)}), f32[18,1024]{1,0:T(8,128)}) %all-reduce.3.cloned.1.call-update) | async-done | bytes 73744 | tf_op jit(solution)/shard_map/psum | solution.py:312
  585.8 14.7 %collective-permute-done.32 = bf16[128,1024]{0,1:T(8,128)(2,1)S(1)} collective-permute-done((bf16[128,1024]{0,1:T(8,128)(2,1)S(1)}, bf16[128,1024]{0,1:T(8,128)(2,1)S(1)}, u32[]{:S(2)}, u32[]{:S(2)}) %collective-permute-start.32) | collective-permute-done | bytes 262176 | tf_op jit(solution)/shard_map/ppermute | solution.py:124
  604.5 16.3 %collective-permute-done.33 = bf16[128,1024]{0,1:T(8,128)(2,1)S(1)} collective-permute-done((bf16[128,1024]{0,1:T(8,128)(2,1)S(1)}, bf16[128,1024]{0,1:T(8,128)(2,1)S(1)}, u32[]{:S(2)}, u32[]{:S(2)}) %collective-permute-start.33) | collective-permute-done | bytes 262176 | tf_op jit(solution)/shard_map/ppermute | solution.py:124
  625.9 47.9 %reduce-scatter.4.cloned.1.call-done = bf16[128,2048]{1,0:T(8,128)(2,1)} async-done(((bf16[1024,2048]{1,0:T(8,128)(2,1)}), bf16[128,2048]{1,0:T(8,128)(2,1)}) %reduce-scatter.4.cloned.1.call-update) | async-done | bytes 524304
  (495 shorter events, 290.1 us)
Async XLA Ops:
  7.2 171.6 %all-gather.2.cloned.1.call-start = ((), (), s32[]{:S(2)}) async-start(), calls=%async_computation.1 | async-start | bytes 4718592 | tf_op jit(solution)/shard_map/all_gather | solution.py:184
  9.1 77.5 %collective-permute-start = (bf16[128,1024]{0,1:T(8,128)(2,1)S(1)}, bf16[128,1024]{0,1:T(8,128)(2,1)}, u32[]{:S(2)}, u32[]{:S(2)}) collective-permute-start(bf16[128,1024]{0,1:T(8,128)(2,1)S(1)} %get-tuple-element.117), channel_id=1, source_target_pairs={{8,0},{16,8},{24,16},{28,24},{20,28},{12,20},{4,12},{0,4},{9,1},{1... | collective-permute-start | bytes 786440 | tf_op jit(solution)/shard_map/ppermute | solution.py:106
  12.1 74.6 %collective-permute-start.1 = (bf16[128,1024]{0,1:T(8,128)(2,1)S(1)}, bf16[128,1024]{0,1:T(8,128)(2,1)S(1)}, u32[]{:S(2)}, u32[]{:S(2)}) collective-permute-start(bf16[128,1024]{0,1:T(8,128)(2,1)S(1)} %get-tuple-element.117), channel_id=1, source_target_pairs={{0,8},{8,16},{16,24},{24,28},{28,20},{20,12},{12,4},{4,0},{1,9},{9... | collective-permute-start | bytes 786440 | tf_op jit(solution)/shard_map/ppermute | solution.py:104
  13.3 556.8 %all-reduce.3.cloned.1.call-start = ((), (), s32[]{:S(2)}) async-start(), calls=%async_computation.2 | async-start | bytes 196608 | tf_op jit(solution)/shard_map/psum | solution.py:312
  86.6 17.2 %collective-permute-start.2 = (bf16[128,1024]{0,1:T(8,128)(2,1)}, bf16[128,1024]{0,1:T(8,128)(2,1)}, u32[]{:S(2)}, u32[]{:S(2)}) collective-permute-start(bf16[128,1024]{0,1:T(8,128)(2,1)} %collective-permute-done), channel_id=1, source_target_pairs={{8,0},{16,8},{24,16},{28,24},{20,28},{12,20},{4,12},{0,4},{9,1},{1... | collective-permute-start | bytes 786440 | tf_op jit(solution)/shard_map/ppermute | solution.py:106
  86.6 15.7 %collective-permute-start.3 = (bf16[128,1024]{0,1:T(8,128)(2,1)S(1)}, bf16[128,1024]{0,1:T(8,128)(2,1)}, u32[]{:S(2)}, u32[]{:S(2)}) collective-permute-start(bf16[128,1024]{0,1:T(8,128)(2,1)S(1)} %collective-permute-done.1), channel_id=1, source_target_pairs={{0,8},{8,16},{16,24},{24,28},{28,20},{20,12},{12,4},{4,0},{1,9},{9... | collective-permute-start | bytes 786440 | tf_op jit(solution)/shard_map/ppermute | solution.py:104
  144.7 25.3 %collective-permute-start.8 = (bf16[512,1024]{1,0:T(8,128)(2,1)S(1)}, bf16[512,1024]{1,0:T(8,128)(2,1)S(1)}, u32[]{:S(2)}, u32[]{:S(2)}) collective-permute-start(bf16[512,1024]{1,0:T(8,128)(2,1)S(1)} %add_convert_fusion.5), channel_id=1, source_target_pairs={{0,2},{1,3},{2,0},{3,1},{4,6},{5,7},{6,4},{7,5},{8,10},{9,11},{10,... | collective-permute-start | bytes 3145736 | tf_op jit(solution)/shard_map/ppermute | solution.py:133
  192.7 25.4 %collective-permute-start.18 = (bf16[512,1024]{1,0:T(8,128)(2,1)S(1)}, bf16[512,1024]{1,0:T(8,128)(2,1)}, u32[]{:S(2)}, u32[]{:S(2)}) collective-permute-start(bf16[512,1024]{1,0:T(8,128)(2,1)S(1)} %add_convert_fusion.1), channel_id=1, source_target_pairs={{0,2},{1,3},{2,0},{3,1},{4,6},{5,7},{6,4},{7,5},{8,10},{9,11},{10,... | collective-permute-start | bytes 3145736 | tf_op jit(solution)/shard_map/ppermute | solution.py:133
  296.9 25.3 %collective-permute-start.13 = (bf16[512,1024]{1,0:T(8,128)(2,1)S(1)}, bf16[512,1024]{1,0:T(8,128)(2,1)S(1)}, u32[]{:S(2)}, u32[]{:S(2)}) collective-permute-start(bf16[512,1024]{1,0:T(8,128)(2,1)S(1)} %add_convert_fusion.3), channel_id=1, source_target_pairs={{0,2},{1,3},{2,0},{3,1},{4,6},{5,7},{6,4},{7,5},{8,10},{9,11},{10,... | collective-permute-start | bytes 3145736 | tf_op jit(solution)/shard_map/ppermute | solution.py:133
  324.3 15.6 %collective-permute-start.14 = (bf16[512,1024]{1,0:T(8,128)(2,1)}, bf16[512,1024]{1,0:T(8,128)(2,1)}, u32[]{:S(2)}, u32[]{:S(2)}) collective-permute-start(bf16[512,1024]{1,0:T(8,128)(2,1)} %multiply_convert_fusion.6), channel_id=1, source_target_pairs={{0,1},{1,0},{2,3},{3,2},{4,5},{5,4},{6,7},{7,6},{8,9},{9,8},{10,11... | collective-permute-start | bytes 3145736 | tf_op jit(solution)/shard_map/ppermute | solution.py:133
  339.5 121.9 %collective-permute-start.10 = (bf16[1024,2,256]{2,0,1:T(8,128)(2,1)}, bf16[1024,2,256]{2,0,1:T(8,128)(2,1)}, u32[]{:S(2)}, u32[]{:S(2)}) collective-permute-start(bf16[1024,2,256]{2,0,1:T(8,128)(2,1)} %fusion.154), channel_id=1, source_target_pairs={{0,1},{1,0},{2,3},{3,2},{4,5},{5,4},{6,7},{7,6},{8,9},{9,8},{10,11... | collective-permute-start | bytes 3145736 | tf_op jit(solution)/shard_map/ppermute | solution.py:133
  365.6 100.3 %collective-permute-start.20 = (bf16[1024,2,256]{2,0,1:T(8,128)(2,1)}, bf16[1024,2,256]{2,0,1:T(8,128)(2,1)}, u32[]{:S(2)}, u32[]{:S(2)}) collective-permute-start(bf16[1024,2,256]{2,0,1:T(8,128)(2,1)} %dynamic-slice_bitcast_fusion.1), channel_id=1, source_target_pairs={{0,1},{1,0},{2,3},{3,2},{4,5},{5,4},{6,7},{7,6},{8,9},{9,8},{10,11... | collective-permute-start | bytes 3145736 | tf_op jit(solution)/shard_map/ppermute | solution.py:133
  370.4 25.7 %collective-permute-start.23 = (bf16[512,1024]{1,0:T(8,128)(2,1)}, bf16[512,1024]{1,0:T(8,128)(2,1)}, u32[]{:S(2)}, u32[]{:S(2)}) collective-permute-start(bf16[512,1024]{1,0:T(8,128)(2,1)} %add_convert_fusion), channel_id=1, source_target_pairs={{0,2},{1,3},{2,0},{3,1},{4,6},{5,7},{6,4},{7,5},{8,10},{9,11},{10,... | collective-permute-start | bytes 3145736 | tf_op jit(solution)/shard_map/ppermute | solution.py:133
  450.2 223.6 %reduce-scatter.4.cloned.1.call-start = ((), (), s32[]{:S(2)}) async-start(), calls=%async_computation.3 | async-start | bytes 4718592
  464.4 15.1 %collective-permute-start.11 = (bf16[1024,1,256]{2,0,1:T(8,128)(2,1)}, bf16[1024,1,256]{2,0,1:T(8,128)(2,1)}, u32[]{:S(2)}, u32[]{:S(2)}) collective-permute-start(bf16[1024,1,256]{2,0,1:T(8,128)(2,1)} %dynamic-slice_convert_fusion.3), channel_id=1, source_target_pairs={{0,2},{1,3},{2,0},{3,1},{4,6},{5,7},{6,4},{7,5},{8,10},{9,11},{10,... | collective-permute-start | bytes 1572872 | tf_op jit(solution)/shard_map/ppermute | solution.py:133
  473.2 23.1 %collective-permute-start.15 = (bf16[1024,2,256]{2,0,1:T(8,128)(2,1)}, bf16[1024,2,256]{2,0,1:T(8,128)(2,1)S(1)}, u32[]{:S(2)}, u32[]{:S(2)}) collective-permute-start(bf16[1024,2,256]{2,0,1:T(8,128)(2,1)} %fusion.150), channel_id=1, source_target_pairs={{0,1},{1,0},{2,3},{3,2},{4,5},{5,4},{6,7},{7,6},{8,9},{9,8},{10,11... | collective-permute-start | bytes 3145736 | tf_op jit(solution)/shard_map/ppermute | solution.py:133
  497.7 80.0 %collective-permute-start.16 = (bf16[1024,1,256]{2,0,1:T(8,128)(2,1)}, bf16[1024,1,256]{2,0,1:T(8,128)(2,1)}, u32[]{:S(2)}, u32[]{:S(2)}) collective-permute-start(bf16[1024,1,256]{2,0,1:T(8,128)(2,1)} %dynamic-slice_convert_fusion.2), channel_id=1, source_target_pairs={{0,2},{1,3},{2,0},{3,1},{4,6},{5,7},{6,4},{7,5},{8,10},{9,11},{10,... | collective-permute-start | bytes 1572872 | tf_op jit(solution)/shard_map/ppermute | solution.py:133
  507.7 71.2 %collective-permute-start.31 = (bf16[128,1024]{0,1:T(8,128)(2,1)}, bf16[128,1024]{0,1:T(8,128)(2,1)S(1)}, u32[]{:S(2)}, u32[]{:S(2)}) collective-permute-start(bf16[128,1024]{0,1:T(8,128)(2,1)} %get-tuple-element.90), channel_id=1, source_target_pairs={{8,0},{16,8},{24,16},{28,24},{20,28},{12,20},{4,12},{0,4},{9,1},{1... | collective-permute-start | bytes 786440 | tf_op jit(solution)/shard_map/ppermute | solution.py:124
  517.4 54.6 %collective-permute-start.28 = (bf16[128,1024]{0,1:T(8,128)(2,1)}, bf16[128,1024]{0,1:T(8,128)(2,1)}, u32[]{:S(2)}, u32[]{:S(2)}) collective-permute-start(bf16[128,1024]{0,1:T(8,128)(2,1)} %add_convert_fusion.12), channel_id=1, source_target_pairs={{0,8},{8,16},{16,24},{24,28},{28,20},{20,12},{12,4},{4,0},{1,9},{9... | collective-permute-start | bytes 786440 | tf_op jit(solution)/shard_map/ppermute | solution.py:124
  520.4 80.2 %collective-permute-start.25 = (bf16[1024,2,256]{2,0,1:T(8,128)(2,1)}, bf16[1024,2,256]{2,0,1:T(8,128)(2,1)S(1)}, u32[]{:S(2)}, u32[]{:S(2)}) collective-permute-start(bf16[1024,2,256]{2,0,1:T(8,128)(2,1)} %dynamic-slice_bitcast_fusion), channel_id=1, source_target_pairs={{0,1},{1,0},{2,3},{3,2},{4,5},{5,4},{6,7},{7,6},{8,9},{9,8},{10,11... | collective-permute-start | bytes 3145736 | tf_op jit(solution)/shard_map/ppermute | solution.py:133
  581.0 19.4 %collective-permute-start.32 = (bf16[128,1024]{0,1:T(8,128)(2,1)S(1)}, bf16[128,1024]{0,1:T(8,128)(2,1)S(1)}, u32[]{:S(2)}, u32[]{:S(2)}) collective-permute-start(bf16[128,1024]{0,1:T(8,128)(2,1)S(1)} %get-tuple-element.88), channel_id=1, source_target_pairs={{8,0},{16,8},{24,16},{28,24},{20,28},{12,20},{4,12},{0,4},{9,1},{1... | collective-permute-start | bytes 786440 | tf_op jit(solution)/shard_map/ppermute | solution.py:124
  585.2 19.2 %collective-permute-start.30 = (bf16[128,1024]{0,1:T(8,128)(2,1)S(1)}, bf16[128,1024]{0,1:T(8,128)(2,1)S(1)}, u32[]{:S(2)}, u32[]{:S(2)}) collective-permute-start(bf16[128,1024]{0,1:T(8,128)(2,1)S(1)} %get-tuple-element.87), channel_id=1, source_target_pairs={{0,8},{8,16},{16,24},{24,28},{28,20},{20,12},{12,4},{4,0},{1,9},{9... | collective-permute-start | bytes 786440 | tf_op jit(solution)/shard_map/ppermute | solution.py:124
  600.5 20.2 %collective-permute-start.33 = (bf16[128,1024]{0,1:T(8,128)(2,1)S(1)}, bf16[128,1024]{0,1:T(8,128)(2,1)S(1)}, u32[]{:S(2)}, u32[]{:S(2)}) collective-permute-start(bf16[128,1024]{0,1:T(8,128)(2,1)S(1)} %add_convert_fusion.8), channel_id=1, source_target_pairs={{8,0},{16,8},{24,16},{28,24},{20,28},{12,20},{4,12},{0,4},{9,1},{1... | collective-permute-start | bytes 786440 | tf_op jit(solution)/shard_map/ppermute | solution.py:124
  602.5 20.1 %collective-permute-start.26 = (bf16[1024,1,256]{2,0,1:T(8,128)(2,1)S(1)}, bf16[1024,1,256]{2,0,1:T(8,128)(2,1)S(1)}, u32[]{:S(2)}, u32[]{:S(2)}) collective-permute-start(bf16[1024,1,256]{2,0,1:T(8,128)(2,1)S(1)} %dynamic-slice_convert_fusion), channel_id=1, source_target_pairs={{0,2},{1,3},{2,0},{3,1},{4,6},{5,7},{6,4},{7,5},{8,10},{9,11},{10,... | collective-permute-start | bytes 1572872 | tf_op jit(solution)/shard_map/ppermute | solution.py:133
  (132 other events, 960.9 us)
Sparse Core Ops, SparseCore 0:
  13.4 80.6 all-gather.1
  450.4 119.6 all-reduce.2
  573.7 100.0 reduce-scatter.3
where the time goes:
time: 692 us; the launch traced here: 684 us
  waiting for transfers between devices  223 us (32%)
  matrix products  145 us (21%)
  other arithmetic  122 us (18%)
  local copies, waits for them, and re-layouts  90.8 us (13%)
  blocking collectives  43.3 us (6%)
  starting transfers between devices  30.4 us (4%)
  between operations  29.9 us (4%)
    ppermute x20, waiting for transfers between devices, swap(): return lax.ppermute(value, 'tensor', [(i, i ^ bit) for i in range(n)])  82.7 us
    psum x1, waiting for transfers between devices, shards(): sums = lax.psum(sums, ('dp', 'tensor'))  49.7 us
    unnamed x4, waiting for transfers between devices  47.9 us
    unnamed x253, local copies, waits for them, and re-layouts  38.4 us
    ppermute x7, waiting for transfers between devices, scatter(): run = lax.ppermute(run.astype(bf16), 'dp', way).astype(f32)  35.6 us
    all_gather x1, blocking collectives, shards(): small = lax.all_gather(small, 'dp', axis=1, tiled=True)  31.2 us
    dot_general x8, matrix products, mm(): return jnp.dot(left, right, preferred_element_type=f32)  26.2 us
    dot_general x4, matrix products, mm_lt(): return jnp.einsum('ki,kj->ij', left, right, preferred_element_type=f32)  25 us
  transfers between devices with their start and end apart: 37, of which 18 were waited for; matrix products, arithmetic and copies ran while one was open for 36% of the time, Pallas kernels for 0%

commit v1 on v0

--- a/solution.py
+++ b/solution.py
@@ -309,7 +309,7 @@
     sums = jnp.zeros((n_seqs, width), f32)
     sums = lax.dynamic_update_slice_in_dim(sums, jnp.stack(seq_sums), me_dp * seqs_dev, 0)
     sums = jnp.concatenate([sums, gain_attn_sum[None], gain_mlp_sum[None] * (1.0 / chips)], axis=0)
-    sums = lax.psum(sums, ("dp", "tensor"))
+    sums = jnp.sum(lax.all_gather(sums, ("dp", "tensor")), axis=0)
     rows = width // n_dp
     sums = lax.dynamic_slice_in_dim(sums, me_dp * rows, rows, 1)
     factor = float(n_seqs * seq_len) ** (-0.5)

time: 692 us -> 604 us (0.87)
  waiting for transfers between devices: 223 us -> 149 us
  matrix products: 145 us -> 138 us
    psum x1 -> x0, waiting for transfers between devices: 49.7 us -> none  [shards(): sums = lax.psum(sums, ('dp', 'tensor'))]
    unnamed x4, waiting for transfers between devices: 47.9 us -> 8.09 us
    ppermute x20, waiting for transfers between devices: 82.7 us -> 100 us  [swap(): return lax.ppermute(value, 'tensor', [(i, i ^ bit) for i in range(n)])]
  transfers between devices with their start and end apart: 37 -> 37, of which waited for: 18 -> 20; matrix products, arithmetic and copies ran while one was open for 36% -> 30% of each run, Pallas kernels for 0% -> 0%
where the time goes in v1:
time: 604 us; the launch traced here: 596 us
  waiting for transfers between devices  149 us (25%)
  matrix products  138 us (23%)
  other arithmetic  118 us (20%)
  local copies, waits for them, and re-layouts  87.1 us (14%)
  blocking collectives  43.3 us (7%)
  starting transfers between devices  30.5 us (5%)
  between operations  30.3 us (5%)
    ppermute x20, waiting for transfers between devices, swap(): return lax.ppermute(value, 'tensor', [(i, i ^ bit) for i in range(n)])  100 us
    unnamed x253, local copies, waits for them, and re-layouts  39.8 us
    ppermute x7, waiting for transfers between devices, scatter(): run = lax.ppermute(run.astype(bf16), 'dp', way).astype(f32)  32.8 us
    all_gather x1, blocking collectives, shards(): small = lax.all_gather(small, 'dp', axis=1, tiled=True)  31.2 us
    dot_general x8, matrix products, mm(): return jnp.dot(left, right, preferred_element_type=f32)  23.7 us
    dot_general x4, matrix products, mm_lt(): return jnp.einsum('ki,kj->ij', left, right, preferred_element_type=f32)  18.9 us
    dot_general x2, matrix products, attend_back(): jnp.einsum('hqk,qhe->khe', probs.astype(bf16), d_mixed, preferred_element...  18.8 us
    dot_general x12, matrix products, mm_rt(): return jnp.einsum('ik,jk->ij', left, right, preferred_element_type=f32)  18.6 us
  transfers between devices with their start and end apart: 37, of which 20 were waited for; matrix products, arithmetic and copies ran while one was open for 30% of the time, Pallas kernels for 0%

profile of v1, /device:TPU:0, one launch (start us, length us, event | category | flops | bytes accessed | tf_op | source)
XLA Modules:
  0.0 596.2 jit_solution(8895811765728366333)
XLA Ops:
  14.9 12.1 %all-reduce = s32[16]{0:T(128)S(1)} all-reduce(s32[16]{0:T(128)S(1)} %dynamic-update-slice), channel_id=1, replica_groups=mesh['dp'=8,'tensor'=4] {'dp'}, use_global_device_ids=true, to_apply=%add | all-reduce | flops 16 | bytes 128
  28.4 31.2 %all_gather.16 = f32[18,1024]{1,0:T(8,128)S(1)} all-gather(f32[18,128]{1,0:T(8,128)S(1)} %pad_maximum_fusion.9), channel_id=1, replica_groups=mesh['dp'=8,'tensor'=4] {'dp'}, dimensions={1}, use_global_device_ids=true | all-gather | bytes 82944 | tf_op jit(solution)/shard_map/all_gather | solution.py:191
  64.4 16.2 %multiply_sine_fusion.1 = (f32[1024,512]{1,0:T(8,128)S(1)}, f32[1024,512]{1,0:T(8,128)S(1)}, f32[1024,512]{1,0:T(8,128)}, f32[1024,512]{1,0:T(8,128)}) fusion(f32[512]{0:T(512)S(1)} %multiply_exponential_fusion, f32[1024]{0:T(1024)S(1)} %get-tuple-element.168, f32[1024]{0:T(1024)S(1)} %get-tuple-element.166), kind=kLoop, calls=%fused_computation.119 | loop fusion | flops 1048576 | bytes 8398848 | tf_op jit(solution)/shard_map/sin | solution.py:19
  117.9 7.5 %fusion.238 = (f32[4,1024]{1,0:T(4,128)S(1)}, f32[4,1024,1024]{1,2,0:T(8,128)}) fusion(bf16[1024,4,64]{0,2,1:T(8,128)(2,1)S(1)} %bitcast.176, bf16[1024,4,64]{0,2,1:T(8,128)(2,1)S(1)} %bitcast.174, pred[1024,1024]{0,1:T(8,128)(4,1)S(1)} %broadcast_compare_fusion.1), kind=kOutput, calls=%fused_computation.439 | convolution fusion | flops 549449728 | bytes 18890752 | tf_op jit(solution)/shard_map/qhe,khe->hqk/dot_general | solution.py:48
  125.3 8.0 %fusion = f32[4,1024]{1,0:T(4,128)S(1)} fusion(f32[4,1024,1024]{1,2,0:T(8,128)} %get-tuple-element.152, f32[4,1024]{1,0:T(4,128)S(1)} %get-tuple-element.151), kind=kLoop, calls=%fused_computation.12 | loop fusion | flops 8384512 | bytes 16809984 | tf_op jit(solution)/shard_map/reduce_sum | solution.py:52
  133.4 7.6 %fusion.144 = bf16[4,64,1024]{2,1,0:T(8,128)(2,1)S(1)} fusion(bf16[1024,4,64]{0,2,1:T(8,128)(2,1)S(1)} %bitcast.188, f32[4,1024,1024]{1,2,0:T(8,128)} %get-tuple-element.152, f32[4,1024]{1,0:T(4,128)S(1)} %fusion, f32[4,1024]{1,0:T(4,128)S(1)} %get-tuple-element.151), kind=kOutput, calls=%fused_computation.250 | convolution fusion | flops 549715968 | bytes 17858560 | tf_op jit(solution)/shard_map/hqk,khe->qhe/dot_general | solution.py:54
  146.2 23.7 %collective-permute-done.8 = bf16[512,1024]{1,0:T(8,128)(2,1)S(1)} collective-permute-done((bf16[512,1024]{1,0:T(8,128)(2,1)S(1)}, bf16[512,1024]{1,0:T(8,128)(2,1)S(1)}, u32[]{:S(2)}, u32[]{:S(2)}) %collective-permute-start.8) | collective-permute-done | bytes 1048608 | tf_op jit(solution)/shard_map/ppermute | solution.py:133
  206.0 11.9 %collective-permute-done.18 = bf16[512,1024]{1,0:T(8,128)(2,1)} collective-permute-done((bf16[512,1024]{1,0:T(8,128)(2,1)S(1)}, bf16[512,1024]{1,0:T(8,128)(2,1)}, u32[]{:S(2)}, u32[]{:S(2)}) %collective-permute-start.18) | collective-permute-done | bytes 1048608 | tf_op jit(solution)/shard_map/ppermute | solution.py:133
  229.0 9.4 %fusion.124 = bf16[4,64,1024]{2,1,0:T(8,128)(2,1)} fusion(bf16[1024,4,64]{0,2,1:T(8,128)(2,1)S(1)} %bitcast.184, f32[4,1024,1024]{1,2,0:T(8,128)} %get-tuple-element.152, f32[4,1024]{1,0:T(4,128)S(1)} %log_add_fusion.1), kind=kOutput, calls=%fused_computation.240 | convolution fusion | flops 545521664 | bytes 17842176 | tf_op jit(solution)/shard_map/hqk,qhe->khe/dot_general | solution.py:63
  238.4 7.6 %multiply_reduce_fusion.1 = (f32[4,1024]{1,0:T(4,128)S(1)}, f32[4,1024,1024]{1,2,0:T(8,128)}) fusion(f32[4,1024,1024]{1,2,0:T(8,128)S(1)} %bitcast.171, f32[4,1024]{1,0:T(4,128)S(1)} %log_add_fusion.1, bf16[1024,4,64]{0,2,1:T(8,128)(2,1)S(1)} %bitcast.185, bf16[1024,4,64]{0,2,1:T(8,128)(2,1)S(1)} %bitcast.189), kind=kOutput, calls=%fused_computation.4 | convolution fusion | flops 549449728 | bytes 34635776 | tf_op jit(solution)/shard_map/qhe,khe->hqk/dot_general | solution.py:62
  246.1 8.3 %multiply_convert_fusion.1 = bf16[4,1024,1024]{1,2,0:T(8,128)(2,1)S(1)} fusion(f32[4,1024,1024]{1,2,0:T(8,128)} %get-tuple-element.156, f32[4,1024,1024]{1,2,0:T(8,128)S(1)} %bitcast.171, f32[4,1024]{1,0:T(4,128)S(1)} %get-tuple-element.155, f32[4,1024]{1,0:T(4,128)S(1)} %log_add_fusion.1), kind=kLoop, calls=%fused_computation.3 | loop fusion | flops 16777216 | bytes 41975808 | tf_op jit(solution)/shard_map/convert_element_type | solution.py:65
  268.9 7.5 %fusion.239 = (f32[4,1024]{1,0:T(4,128)S(1)}, f32[4,1024,1024]{1,2,0:T(8,128)}) fusion(bf16[1024,4,64]{0,2,1:T(8,128)(2,1)S(1)} %bitcast.180, bf16[1024,4,64]{0,2,1:T(8,128)(2,1)S(1)} %bitcast.178, pred[1024,1024]{0,1:T(8,128)(4,1)S(1)} %broadcast_compare_fusion), kind=kOutput, calls=%fused_computation.440 | convolution fusion | flops 549449728 | bytes 18890752 | tf_op jit(solution)/shard_map/qhe,khe->hqk/dot_general | solution.py:48
  276.3 8.0 %fusion.1 = f32[4,1024]{1,0:T(4,128)S(1)} fusion(f32[4,1024,1024]{1,2,0:T(8,128)} %get-tuple-element.159, f32[4,1024]{1,0:T(4,128)S(1)} %get-tuple-element.158), kind=kLoop, calls=%fused_computation.13 | loop fusion | flops 8384512 | bytes 16809984 | tf_op jit(solution)/shard_map/reduce_sum | solution.py:52
  284.4 7.7 %fusion.143 = bf16[4,64,1024]{2,1,0:T(8,128)(2,1)S(1)} fusion(bf16[1024,4,64]{0,2,1:T(8,128)(2,1)S(1)} %bitcast.190, f32[4,1024,1024]{1,2,0:T(8,128)} %get-tuple-element.159, f32[4,1024]{1,0:T(4,128)S(1)} %fusion.1, f32[4,1024]{1,0:T(4,128)S(1)} %get-tuple-element.158), kind=kOutput, calls=%fused_computation.249 | convolution fusion | flops 549715968 | bytes 17858560 | tf_op jit(solution)/shard_map/hqk,khe->qhe/dot_general | solution.py:54
  297.3 23.7 %collective-permute-done.13 = bf16[512,1024]{1,0:T(8,128)(2,1)S(1)} collective-permute-done((bf16[512,1024]{1,0:T(8,128)(2,1)S(1)}, bf16[512,1024]{1,0:T(8,128)(2,1)S(1)}, u32[]{:S(2)}, u32[]{:S(2)}) %collective-permute-start.13) | collective-permute-done | bytes 1048608 | tf_op jit(solution)/shard_map/ppermute | solution.py:133
  349.8 15.2 %collective-permute-done.23 = bf16[512,1024]{1,0:T(8,128)(2,1)} collective-permute-done((bf16[512,1024]{1,0:T(8,128)(2,1)}, bf16[512,1024]{1,0:T(8,128)(2,1)}, u32[]{:S(2)}, u32[]{:S(2)}) %collective-permute-start.23) | collective-permute-done | bytes 1048608 | tf_op jit(solution)/shard_map/ppermute | solution.py:133
  379.7 9.4 %fusion.127 = bf16[4,64,1024]{2,1,0:T(8,128)(2,1)} fusion(bf16[1024,4,64]{0,2,1:T(8,128)(2,1)S(1)} %bitcast.186, f32[4,1024,1024]{1,2,0:T(8,128)} %get-tuple-element.159, f32[4,1024]{1,0:T(4,128)S(1)} %log_add_fusion), kind=kOutput, calls=%fused_computation.241 | convolution fusion | flops 545521664 | bytes 17842176 | tf_op jit(solution)/shard_map/hqk,qhe->khe/dot_general | solution.py:63
  389.1 10.5 %multiply_reduce_fusion = (f32[4,1024]{1,0:T(4,128)S(1)}, f32[4,1024,1024]{1,2,0:T(8,128)}) fusion(f32[4,1024,1024]{1,2,0:T(8,128)S(1)} %bitcast.173, f32[4,1024]{1,0:T(4,128)S(1)} %log_add_fusion, bf16[1024,4,64]{0,2,1:T(8,128)(2,1)} %bitcast.187, bf16[1024,4,64]{0,2,1:T(8,128)(2,1)} %bitcast.191), kind=kOutput, calls=%fused_computation.1 | convolution fusion | flops 549449728 | bytes 34635776 | tf_op jit(solution)/shard_map/qhe,khe->hqk/dot_general | solution.py:62
  399.7 8.3 %multiply_convert_fusion = bf16[4,1024,1024]{1,2,0:T(8,128)(2,1)S(1)} fusion(f32[4,1024,1024]{1,2,0:T(8,128)} %get-tuple-element.163, f32[4,1024,1024]{1,2,0:T(8,128)S(1)} %bitcast.173, f32[4,1024]{1,0:T(4,128)S(1)} %get-tuple-element.162, f32[4,1024]{1,0:T(4,128)S(1)} %log_add_fusion), kind=kLoop, calls=%fused_computation | loop fusion | flops 16777216 | bytes 41975808 | tf_op jit(solution)/shard_map/convert_element_type | solution.py:65
  452.8 6.7 %copy.139 = bf16[1024,2048]{1,0:T(8,128)(2,1)} copy(bf16[1024,2048]{0,1:T(8,128)(2,1)} %pad_maximum_fusion) | data formatting | bytes 8388608
  484.4 7.2 %collective-permute-done.21 = bf16[1024,1,256]{2,0,1:T(8,128)(2,1)} collective-permute-done((bf16[1024,1,256]{2,0,1:T(8,128)(2,1)S(1)}, bf16[1024,1,256]{2,0,1:T(8,128)(2,1)}, u32[]{:S(2)}, u32[]{:S(2)}) %collective-permute-start.21) | collective-permute-done | bytes 524320 | tf_op jit(solution)/shard_map/ppermute | solution.py:133
  529.1 10.5 %collective-permute-done.28 = bf16[128,1024]{0,1:T(8,128)(2,1)S(1)} collective-permute-done((bf16[128,1024]{0,1:T(8,128)(2,1)S(1)}, bf16[128,1024]{0,1:T(8,128)(2,1)S(1)}, u32[]{:S(2)}, u32[]{:S(2)}) %collective-permute-start.28) | collective-permute-done | bytes 262176 | tf_op jit(solution)/shard_map/ppermute | solution.py:124
  542.5 9.2 %collective-permute-done.29 = bf16[128,1024]{0,1:T(8,128)(2,1)S(1)} collective-permute-done((bf16[128,1024]{0,1:T(8,128)(2,1)S(1)}, bf16[128,1024]{0,1:T(8,128)(2,1)S(1)}, u32[]{:S(2)}, u32[]{:S(2)}) %collective-permute-start.29) | collective-permute-done | bytes 262176 | tf_op jit(solution)/shard_map/ppermute | solution.py:124
  577.9 8.0 %reduce-scatter.4.cloned.1.call-done = bf16[128,2048]{1,0:T(8,128)(2,1)} async-done(((bf16[1024,2048]{1,0:T(8,128)(2,1)}), bf16[128,2048]{1,0:T(8,128)(2,1)}) %reduce-scatter.4.cloned.1.call-update) | async-done | bytes 524304
  (496 shorter events, 290.5 us)
Async XLA Ops:
  7.2 171.6 %all-gather.5.cloned.1.call-start = ((), (), s32[]{:S(2)}) async-start(), calls=%async_computation.1 | async-start | bytes 4718592 | tf_op jit(solution)/shard_map/all_gather | solution.py:184
  9.1 77.4 %collective-permute-start = (bf16[128,1024]{0,1:T(8,128)(2,1)S(1)}, bf16[128,1024]{0,1:T(8,128)(2,1)}, u32[]{:S(2)}, u32[]{:S(2)}) collective-permute-start(bf16[128,1024]{0,1:T(8,128)(2,1)S(1)} %get-tuple-element.117), channel_id=1, source_target_pairs={{8,0},{16,8},{24,16},{28,24},{20,28},{12,20},{4,12},{0,4},{9,1},{1... | collective-permute-start | bytes 786440 | tf_op jit(solution)/shard_map/ppermute | solution.py:106
  12.1 74.4 %collective-permute-start.1 = (bf16[128,1024]{0,1:T(8,128)(2,1)S(1)}, bf16[128,1024]{0,1:T(8,128)(2,1)S(1)}, u32[]{:S(2)}, u32[]{:S(2)}) collective-permute-start(bf16[128,1024]{0,1:T(8,128)(2,1)S(1)} %get-tuple-element.117), channel_id=1, source_target_pairs={{0,8},{8,16},{16,24},{24,28},{28,20},{20,12},{12,4},{4,0},{1,9},{9... | collective-permute-start | bytes 786440 | tf_op jit(solution)/shard_map/ppermute | solution.py:104
  13.3 560.8 %all-gather.7.cloned.1.call-start = ((), (), s32[]{:S(2)}) async-start(), calls=%async_computation.2 | async-start | bytes 3244032 | tf_op jit(solution)/shard_map/all_gather | solution.py:312
  86.5 17.2 %collective-permute-start.2 = (bf16[128,1024]{0,1:T(8,128)(2,1)}, bf16[128,1024]{0,1:T(8,128)(2,1)}, u32[]{:S(2)}, u32[]{:S(2)}) collective-permute-start(bf16[128,1024]{0,1:T(8,128)(2,1)} %collective-permute-done), channel_id=1, source_target_pairs={{8,0},{16,8},{24,16},{28,24},{20,28},{12,20},{4,12},{0,4},{9,1},{1... | collective-permute-start | bytes 786440 | tf_op jit(solution)/shard_map/ppermute | solution.py:106
  86.5 15.7 %collective-permute-start.3 = (bf16[128,1024]{0,1:T(8,128)(2,1)S(1)}, bf16[128,1024]{0,1:T(8,128)(2,1)}, u32[]{:S(2)}, u32[]{:S(2)}) collective-permute-start(bf16[128,1024]{0,1:T(8,128)(2,1)S(1)} %collective-permute-done.1), channel_id=1, source_target_pairs={{0,8},{8,16},{16,24},{24,28},{28,20},{20,12},{12,4},{4,0},{1,9},{9... | collective-permute-start | bytes 786440 | tf_op jit(solution)/shard_map/ppermute | solution.py:104
  144.6 25.3 %collective-permute-start.8 = (bf16[512,1024]{1,0:T(8,128)(2,1)S(1)}, bf16[512,1024]{1,0:T(8,128)(2,1)S(1)}, u32[]{:S(2)}, u32[]{:S(2)}) collective-permute-start(bf16[512,1024]{1,0:T(8,128)(2,1)S(1)} %add_convert_fusion.5), channel_id=1, source_target_pairs={{0,2},{1,3},{2,0},{3,1},{4,6},{5,7},{6,4},{7,5},{8,10},{9,11},{10,... | collective-permute-start | bytes 3145736 | tf_op jit(solution)/shard_map/ppermute | solution.py:133
  192.6 25.4 %collective-permute-start.18 = (bf16[512,1024]{1,0:T(8,128)(2,1)S(1)}, bf16[512,1024]{1,0:T(8,128)(2,1)}, u32[]{:S(2)}, u32[]{:S(2)}) collective-permute-start(bf16[512,1024]{1,0:T(8,128)(2,1)S(1)} %add_convert_fusion.1), channel_id=1, source_target_pairs={{0,2},{1,3},{2,0},{3,1},{4,6},{5,7},{6,4},{7,5},{8,10},{9,11},{10,... | collective-permute-start | bytes 3145736 | tf_op jit(solution)/shard_map/ppermute | solution.py:133
  295.7 25.3 %collective-permute-start.13 = (bf16[512,1024]{1,0:T(8,128)(2,1)S(1)}, bf16[512,1024]{1,0:T(8,128)(2,1)S(1)}, u32[]{:S(2)}, u32[]{:S(2)}) collective-permute-start(bf16[512,1024]{1,0:T(8,128)(2,1)S(1)} %add_convert_fusion.3), channel_id=1, source_target_pairs={{0,2},{1,3},{2,0},{3,1},{4,6},{5,7},{6,4},{7,5},{8,10},{9,11},{10,... | collective-permute-start | bytes 3145736 | tf_op jit(solution)/shard_map/ppermute | solution.py:133
  339.5 25.5 %collective-permute-start.23 = (bf16[512,1024]{1,0:T(8,128)(2,1)}, bf16[512,1024]{1,0:T(8,128)(2,1)}, u32[]{:S(2)}, u32[]{:S(2)}) collective-permute-start(bf16[512,1024]{1,0:T(8,128)(2,1)} %add_convert_fusion), channel_id=1, source_target_pairs={{0,2},{1,3},{2,0},{3,1},{4,6},{5,7},{6,4},{7,5},{8,10},{9,11},{10,... | collective-permute-start | bytes 3145736 | tf_op jit(solution)/shard_map/ppermute | solution.py:133
  420.4 165.5 %reduce-scatter.4.cloned.1.call-start = ((), (), s32[]{:S(2)}) async-start(), calls=%async_computation.3 | async-start | bytes 4718592
  425.0 34.5 %collective-permute-start.10 = (bf16[1024,2,256]{2,0,1:T(8,128)(2,1)}, bf16[1024,2,256]{2,0,1:T(8,128)(2,1)}, u32[]{:S(2)}, u32[]{:S(2)}) collective-permute-start(bf16[1024,2,256]{2,0,1:T(8,128)(2,1)} %fusion.154), channel_id=1, source_target_pairs={{0,1},{1,0},{2,3},{3,2},{4,5},{5,4},{6,7},{7,6},{8,9},{9,8},{10,11... | collective-permute-start | bytes 3145736 | tf_op jit(solution)/shard_map/ppermute | solution.py:133
  436.8 26.8 %collective-permute-start.20 = (bf16[1024,2,256]{2,0,1:T(8,128)(2,1)}, bf16[1024,2,256]{2,0,1:T(8,128)(2,1)S(1)}, u32[]{:S(2)}, u32[]{:S(2)}) collective-permute-start(bf16[1024,2,256]{2,0,1:T(8,128)(2,1)} %dynamic-slice_bitcast_fusion.1), channel_id=1, source_target_pairs={{0,1},{1,0},{2,3},{3,2},{4,5},{5,4},{6,7},{7,6},{8,9},{9,8},{10,11... | collective-permute-start | bytes 3145736 | tf_op jit(solution)/shard_map/ppermute | solution.py:133
  462.2 18.5 %collective-permute-start.11 = (bf16[1024,1,256]{2,0,1:T(8,128)(2,1)}, bf16[1024,1,256]{2,0,1:T(8,128)(2,1)}, u32[]{:S(2)}, u32[]{:S(2)}) collective-permute-start(bf16[1024,1,256]{2,0,1:T(8,128)(2,1)} %dynamic-slice_convert_fusion.3), channel_id=1, source_target_pairs={{0,2},{1,3},{2,0},{3,1},{4,6},{5,7},{6,4},{7,5},{8,10},{9,11},{10,... | collective-permute-start | bytes 1572872 | tf_op jit(solution)/shard_map/ppermute | solution.py:133
  469.6 25.9 %collective-permute-start.15 = (bf16[1024,2,256]{2,0,1:T(8,128)(2,1)}, bf16[1024,2,256]{2,0,1:T(8,128)(2,1)}, u32[]{:S(2)}, u32[]{:S(2)}) collective-permute-start(bf16[1024,2,256]{2,0,1:T(8,128)(2,1)} %fusion.150), channel_id=1, source_target_pairs={{0,1},{1,0},{2,3},{3,2},{4,5},{5,4},{6,7},{7,6},{8,9},{9,8},{10,11... | collective-permute-start | bytes 3145736 | tf_op jit(solution)/shard_map/ppermute | solution.py:133
  472.6 19.0 %collective-permute-start.21 = (bf16[1024,1,256]{2,0,1:T(8,128)(2,1)S(1)}, bf16[1024,1,256]{2,0,1:T(8,128)(2,1)}, u32[]{:S(2)}, u32[]{:S(2)}) collective-permute-start(bf16[1024,1,256]{2,0,1:T(8,128)(2,1)S(1)} %dynamic-slice_convert_fusion.1), channel_id=1, source_target_pairs={{0,2},{1,3},{2,0},{3,1},{4,6},{5,7},{6,4},{7,5},{8,10},{9,11},{10,... | collective-permute-start | bytes 1572872 | tf_op jit(solution)/shard_map/ppermute | solution.py:133
  498.1 43.2 %collective-permute-start.16 = (bf16[1024,1,256]{2,0,1:T(8,128)(2,1)}, bf16[1024,1,256]{2,0,1:T(8,128)(2,1)}, u32[]{:S(2)}, u32[]{:S(2)}) collective-permute-start(bf16[1024,1,256]{2,0,1:T(8,128)(2,1)} %dynamic-slice_convert_fusion.2), channel_id=1, source_target_pairs={{0,2},{1,3},{2,0},{3,1},{4,6},{5,7},{6,4},{7,5},{8,10},{9,11},{10,... | collective-permute-start | bytes 1572872 | tf_op jit(solution)/shard_map/ppermute | solution.py:133
  507.9 13.7 %collective-permute-start.27 = (bf16[128,1024]{0,1:T(8,128)(2,1)}, bf16[128,1024]{0,1:T(8,128)(2,1)}, u32[]{:S(2)}, u32[]{:S(2)}) collective-permute-start(bf16[128,1024]{0,1:T(8,128)(2,1)} %get-tuple-element.89), channel_id=1, source_target_pairs={{0,8},{8,16},{16,24},{24,28},{28,20},{20,12},{12,4},{4,0},{1,9},{9... | collective-permute-start | bytes 786440 | tf_op jit(solution)/shard_map/ppermute | solution.py:124
  509.5 33.0 %collective-permute-start.31 = (bf16[128,1024]{0,1:T(8,128)(2,1)}, bf16[128,1024]{0,1:T(8,128)(2,1)S(1)}, u32[]{:S(2)}, u32[]{:S(2)}) collective-permute-start(bf16[128,1024]{0,1:T(8,128)(2,1)} %get-tuple-element.90), channel_id=1, source_target_pairs={{8,0},{16,8},{24,16},{28,24},{20,28},{12,20},{4,12},{0,4},{9,1},{1... | collective-permute-start | bytes 786440 | tf_op jit(solution)/shard_map/ppermute | solution.py:124
  522.6 17.1 %collective-permute-start.28 = (bf16[128,1024]{0,1:T(8,128)(2,1)S(1)}, bf16[128,1024]{0,1:T(8,128)(2,1)S(1)}, u32[]{:S(2)}, u32[]{:S(2)}) collective-permute-start(bf16[128,1024]{0,1:T(8,128)(2,1)S(1)} %add_convert_fusion.12), channel_id=1, source_target_pairs={{0,8},{8,16},{16,24},{24,28},{28,20},{20,12},{12,4},{4,0},{1,9},{9... | collective-permute-start | bytes 786440 | tf_op jit(solution)/shard_map/ppermute | solution.py:124
  529.0 32.0 %collective-permute-start.25 = (bf16[1024,2,256]{2,0,1:T(8,128)(2,1)S(1)}, bf16[1024,2,256]{2,0,1:T(8,128)(2,1)S(1)}, u32[]{:S(2)}, u32[]{:S(2)}) collective-permute-start(bf16[1024,2,256]{2,0,1:T(8,128)(2,1)S(1)} %dynamic-slice_bitcast_fusion), channel_id=1, source_target_pairs={{0,1},{1,0},{2,3},{3,2},{4,5},{5,4},{6,7},{7,6},{8,9},{9,8},{10,11... | collective-permute-start | bytes 3145736 | tf_op jit(solution)/shard_map/ppermute | solution.py:133
  539.7 11.9 %collective-permute-start.29 = (bf16[128,1024]{0,1:T(8,128)(2,1)S(1)}, bf16[128,1024]{0,1:T(8,128)(2,1)S(1)}, u32[]{:S(2)}, u32[]{:S(2)}) collective-permute-start(bf16[128,1024]{0,1:T(8,128)(2,1)S(1)} %add_convert_fusion.11), channel_id=1, source_target_pairs={{0,8},{8,16},{16,24},{24,28},{28,20},{20,12},{12,4},{4,0},{1,9},{9... | collective-permute-start | bytes 786440 | tf_op jit(solution)/shard_map/ppermute | solution.py:124
  551.8 9.0 %collective-permute-start.32 = (bf16[128,1024]{0,1:T(8,128)(2,1)S(1)}, bf16[128,1024]{0,1:T(8,128)(2,1)S(1)}, u32[]{:S(2)}, u32[]{:S(2)}) collective-permute-start(bf16[128,1024]{0,1:T(8,128)(2,1)S(1)} %get-tuple-element.88), channel_id=1, source_target_pairs={{8,0},{16,8},{24,16},{28,24},{20,28},{12,20},{4,12},{0,4},{9,1},{1... | collective-permute-start | bytes 786440 | tf_op jit(solution)/shard_map/ppermute | solution.py:124
  561.5 9.2 %collective-permute-start.26 = (bf16[1024,1,256]{2,0,1:T(8,128)(2,1)S(1)}, bf16[1024,1,256]{2,0,1:T(8,128)(2,1)S(1)}, u32[]{:S(2)}, u32[]{:S(2)}) collective-permute-start(bf16[1024,1,256]{2,0,1:T(8,128)(2,1)S(1)} %dynamic-slice_convert_fusion), channel_id=1, source_target_pairs={{0,2},{1,3},{2,0},{3,1},{4,6},{5,7},{6,4},{7,5},{8,10},{9,11},{10,... | collective-permute-start | bytes 1572872 | tf_op jit(solution)/shard_map/ppermute | solution.py:133
  (132 other events, 874.1 us)
Sparse Core Ops, SparseCore 0:
  13.4 80.4 all-gather.4
  420.5 61.3 all-gather.6
  485.5 100.3 reduce-scatter.3
